TPU v7x, 32 devices: a whole 2x2x4 slice. The times are simulated.
32 devices in a mesh: dp: 8 (over y, x, core), tensor: 4 (over z).
Axes of the slice: x: 2, y: 2, z: 4, core: 2. Of those that a mesh axis runs over, the one named last changes fastest.
Arguments:
- inputs: bfloat16 [768, 32768], P('tensor', 'dp'), may hold values from -18 to 18
- cotangent: float32 [768, 32768], P('tensor', 'dp'), may hold values from -18 to 18
- query_w: bfloat16 [768, 192], P('tensor'), may hold values from -0.21875 to 0.21875
- key_w: bfloat16 [768, 192], P('tensor'), may hold values from -0.21875 to 0.21875
- value_w: bfloat16 [768, 192], P('tensor'), may hold values from -0.4375 to 0.4375
- query_b: float32 [768], P('tensor'), may hold values from -1.75 to 1.75
- value_b: float32 [768], P('tensor'), may hold values from -0.0625 to 0.0625
- output_w: bfloat16 [768, 768], P(None, 'tensor'), may hold values from -4 to 4
- output_b: float32 [768], P('tensor'), may hold values from -1.25 to 1.25
- first_gain: float32 [768], P('tensor'), may hold values from 0.5 to 1.5
- first_shift: float32 [768], P('tensor'), may hold values from -1.25 to 1.25
- inner_w: bfloat16 [3072, 192], P('tensor'), may hold values from -0.4375 to 0.4375
- inner_b: float32 [3072], P('tensor'), may hold values from -1.25 to 1.25
- outer_w: bfloat16 [768, 768], P('tensor'), may hold values from -0.21875 to 0.21875
- outer_b: float32 [768], P('tensor'), may hold values from -1.25 to 1.25
- second_gain: float32 [768], P('tensor'), may hold values from 0.5 to 1.5
- second_shift: float32 [768], P('tensor'), may hold values from -1.25 to 1.25
Outputs:
- layer_out: bfloat16 [768, 32768], P('tensor', 'dp')
- input_grad: bfloat16 [768, 32768], P('tensor', 'dp')
- grad_query_w: float32 [768, 192], P('tensor')
- grad_key_w: float32 [768, 192], P('tensor')
- grad_value_w: float32 [768, 192], P('tensor')
- grad_query_b: float32 [768], P('tensor')
- grad_value_b: float32 [768], P('tensor')
- grad_output_w: float32 [768, 768], P(None, 'tensor')
- grad_output_b: float32 [768], P('tensor')
- grad_first_gain: float32 [768], P('tensor')
- grad_first_shift: float32 [768], P('tensor')
- grad_inner_w: float32 [3072, 192], P('tensor')
- grad_inner_b: float32 [3072], P('tensor')
- grad_outer_w: float32 [768, 768], P('tensor')
- grad_outer_b: float32 [768], P('tensor')
- grad_second_gain: float32 [768], P('tensor')
- grad_second_shift: float32 [768], P('tensor')
All inputs are finite; a program needn't handle non-finite values.
Results may differ from a plain program's by a relative error of at most 0.0095.
Values may be sent and summed in bfloat16 or wider, within the bound.
No kernel may reach another device: no remote copies, remote signals or barrier semaphores. Data moves between devices by JAX's collectives and lax.ppermute only.
A program may use at most 128 MiB of HBM per device.

v0:
```python
from functools import partial
import jax
import jax.numpy as jnp
from jax import lax
from jax.sharding import PartitionSpec as P

D = 768
HDIM = 64
SEQ_LEN = 1024
QBLOCK = 512
EPSILON = 1e-05


def contract_tokens(left, right):
    return lax.dot_general(
        left, right, (((1,), (1,)), ((), ())), preferred_element_type=jnp.float32
    )


def through_weight(weight, grad):
    return lax.dot_general(
        weight, grad, (((0,), (0,)), ((), ())), preferred_element_type=jnp.float32
    )


def per_sequence(array, heads_here):
    number = array.shape[1] // SEQ_LEN
    return jnp.moveaxis(array.reshape(heads_here, HDIM, number, SEQ_LEN), 2, 0)


def to_channels(array):
    number, heads_here = (array.shape[0], array.shape[1])
    return jnp.moveaxis(array, 0, 2).reshape(heads_here * HDIM, number * SEQ_LEN)


def by_blocks(array):
    return jnp.moveaxis(
        array.reshape(array.shape[0], array.shape[1], SEQ_LEN // QBLOCK, QBLOCK), 2, 0
    )


def from_blocks(array):
    return jnp.moveaxis(array, 0, 2).reshape(array.shape[1], array.shape[2], SEQ_LEN)


def attend_forward(triple):
    query, keys, values = triple
    scale = HDIM ** (-0.5)

    def one_block(query_part):
        scores = (
            jnp.einsum("hdq,hdk->hqk", query_part, keys, preferred_element_type=jnp.float32) * scale
        )
        highest = jnp.max(scores, axis=-1, keepdims=True)
        expo = jnp.exp(scores - highest)
        totals = jnp.sum(expo, axis=-1, keepdims=True)
        probs_low = (expo / totals).astype(jnp.bfloat16)
        context = jnp.einsum("hqk,hdk->hdq", probs_low, values, preferred_element_type=jnp.float32)
        return (context, jnp.swapaxes(highest, 1, 2), jnp.swapaxes(totals, 1, 2))

    context, highest, totals = lax.map(one_block, by_blocks(query))
    return (from_blocks(context), from_blocks(highest), from_blocks(totals))


def attend_backward(sextet):
    query, keys, values, grad_context, highest, totals = sextet
    scale = HDIM ** (-0.5)

    def one_block(carry, block):
        grad_keys, grad_values = carry
        query_part, grad_part, high_part, total_part = block
        scores = (
            jnp.einsum("hdq,hdk->hqk", query_part, keys, preferred_element_type=jnp.float32) * scale
        )
        probs = jnp.exp(scores - jnp.swapaxes(high_part, 1, 2)) / jnp.swapaxes(total_part, 1, 2)
        probs_low = probs.astype(jnp.bfloat16)
        grad_probs = jnp.einsum(
            "hdq,hdk->hqk", grad_part, values, preferred_element_type=jnp.float32
        )
        inner_sum = jnp.sum(probs * grad_probs, axis=-1, keepdims=True)
        grad_scores = (probs * (grad_probs - inner_sum)).astype(jnp.bfloat16)
        grad_query = (
            jnp.einsum("hqk,hdk->hdq", grad_scores, keys, preferred_element_type=jnp.float32)
            * scale
        )
        grad_keys = (
            grad_keys
            + jnp.einsum(
                "hqk,hdq->hdk", grad_scores, query_part, preferred_element_type=jnp.float32
            )
            * scale
        )
        grad_values = grad_values + jnp.einsum(
            "hqk,hdq->hdk", probs_low, grad_part, preferred_element_type=jnp.float32
        )
        return ((grad_keys, grad_values), grad_query)

    zeros = jnp.zeros(keys.shape, jnp.float32)
    (grad_keys, grad_values), grad_query = lax.scan(
        one_block,
        (zeros, zeros),
        (by_blocks(query), by_blocks(grad_context), by_blocks(highest), by_blocks(totals)),
    )
    return (from_blocks(grad_query), grad_keys, grad_values)


def norm_backward(grad_hidden, gain, normed, inv_std, sums):
    scaled = grad_hidden * gain[:, None]
    return inv_std * (scaled - sums[0] / D - normed * (sums[1] / D))


def shards(
    inputs,
    cotangent,
    query_w,
    key_w,
    value_w,
    query_b,
    value_b,
    output_w,
    output_b,
    first_gain,
    first_shift,
    inner_w,
    inner_b,
    outer_w,
    outer_b,
    second_gain,
    second_shift,
):
    local = inputs.shape[0]
    tokens = inputs.shape[1]
    heads_here = local // HDIM
    query = (
        jnp.dot(query_w, inputs, preferred_element_type=jnp.float32) + query_b[:, None]
    ).astype(jnp.bfloat16)
    keys = jnp.dot(key_w, inputs, preferred_element_type=jnp.float32).astype(jnp.bfloat16)
    values = (
        jnp.dot(value_w, inputs, preferred_element_type=jnp.float32) + value_b[:, None]
    ).astype(jnp.bfloat16)
    query_seq = per_sequence(query, heads_here)
    keys_seq = per_sequence(keys, heads_here)
    values_seq = per_sequence(values, heads_here)
    context, highest, totals = lax.map(attend_forward, (query_seq, keys_seq, values_seq))
    context_low = to_channels(context).astype(jnp.bfloat16)
    attended = lax.psum_scatter(
        jnp.dot(output_w, context_low, preferred_element_type=jnp.float32),
        "tensor",
        scatter_dimension=0,
        tiled=True,
    )
    first_resid = inputs.astype(jnp.float32) + attended + output_b[:, None]
    first_center = lax.psum(jnp.sum(first_resid, axis=0), "tensor") / D
    first_offset = first_resid - first_center
    first_spread = lax.psum(jnp.sum(first_offset * first_offset, axis=0), "tensor") / D
    first_inv = lax.rsqrt(first_spread + EPSILON)
    first_normed = first_offset * first_inv
    first_hidden = first_normed * first_gain[:, None] + first_shift[:, None]
    hidden_low = first_hidden.astype(jnp.bfloat16)
    inner = jnp.dot(inner_w, hidden_low, preferred_element_type=jnp.float32) + inner_b[:, None]
    activ, gelu_pull = jax.vjp(partial(jax.nn.gelu, approximate=False), inner)
    act_low = activ.astype(jnp.bfloat16)
    second_resid = (
        first_hidden
        + jnp.dot(outer_w, act_low, preferred_element_type=jnp.float32)
        + outer_b[:, None]
    )
    second_center = lax.psum(jnp.sum(second_resid, axis=0), "tensor") / D
    second_offset = second_resid - second_center
    second_spread = lax.psum(jnp.sum(second_offset * second_offset, axis=0), "tensor") / D
    second_inv = lax.rsqrt(second_spread + EPSILON)
    second_normed = second_offset * second_inv
    layer_out = (second_normed * second_gain[:, None] + second_shift[:, None]).astype(jnp.bfloat16)
    grad_second_gain = jnp.sum(cotangent * second_normed, axis=1)
    grad_second_shift = jnp.sum(cotangent, axis=1)
    second_scaled = cotangent * second_gain[:, None]
    second_sums_back = (
        lax.psum(jnp.sum(second_scaled, axis=0).astype(jnp.bfloat16), "tensor").astype(jnp.float32),
        lax.psum(
            jnp.sum(second_scaled * second_normed, axis=0).astype(jnp.bfloat16), "tensor"
        ).astype(jnp.float32),
    )
    grad_second_resid = norm_backward(
        cotangent, second_gain, second_normed, second_inv, second_sums_back
    )
    outer_grad_low = grad_second_resid.astype(jnp.bfloat16)
    grad_outer_b = jnp.sum(outer_grad_low.astype(jnp.float32), axis=1)
    grad_outer_w = contract_tokens(outer_grad_low, act_low)
    grad_act = through_weight(outer_w, outer_grad_low)
    inner_grad_low = gelu_pull(grad_act)[0].astype(jnp.bfloat16)
    grad_inner_b = jnp.sum(inner_grad_low.astype(jnp.float32), axis=1)
    grad_inner_w = contract_tokens(inner_grad_low, hidden_low)
    grad_first_hidden = grad_second_resid + through_weight(inner_w, inner_grad_low)
    grad_first_gain = jnp.sum(grad_first_hidden * first_normed, axis=1)
    grad_first_shift = jnp.sum(grad_first_hidden, axis=1)
    first_scaled = grad_first_hidden * first_gain[:, None]
    first_sums_back = (
        lax.psum(jnp.sum(first_scaled, axis=0).astype(jnp.bfloat16), "tensor").astype(jnp.float32),
        lax.psum(
            jnp.sum(first_scaled * first_normed, axis=0).astype(jnp.bfloat16), "tensor"
        ).astype(jnp.float32),
    )
    grad_first_resid = norm_backward(
        grad_first_hidden, first_gain, first_normed, first_inv, first_sums_back
    )
    attended_grad_low = grad_first_resid.astype(jnp.bfloat16)
    grad_output_b = jnp.sum(attended_grad_low.astype(jnp.float32), axis=1)
    piece = lax.all_gather(attended_grad_low, "tensor", axis=0, tiled=True)
    start = jnp.int32(0)
    weight_rows = lax.dynamic_slice_in_dim(output_w, start, piece.shape[0], 0)
    grad_ctx = jnp.zeros((local, tokens), jnp.float32) + through_weight(weight_rows, piece)
    grad_weight = lax.dynamic_update_slice_in_dim(
        jnp.zeros(output_w.shape, jnp.float32), contract_tokens(piece, context_low), start, 0
    )
    context_grad_low = per_sequence(grad_ctx.astype(jnp.bfloat16), heads_here)
    grad_query, grad_keys, grad_values = lax.map(
        attend_backward, (query_seq, keys_seq, values_seq, context_grad_low, highest, totals)
    )
    query_grad_low = to_channels(grad_query).astype(jnp.bfloat16)
    keys_grad_low = to_channels(grad_keys).astype(jnp.bfloat16)
    values_grad_low = to_channels(grad_values).astype(jnp.bfloat16)
    grad_query_w = contract_tokens(query_grad_low, inputs)
    grad_key_w = contract_tokens(keys_grad_low, inputs)
    grad_value_w = contract_tokens(values_grad_low, inputs)
    grad_query_b = jnp.sum(query_grad_low.astype(jnp.float32), axis=1)
    grad_value_b = jnp.sum(values_grad_low.astype(jnp.float32), axis=1)
    input_grad = (
        grad_first_resid
        + through_weight(query_w, query_grad_low)
        + through_weight(key_w, keys_grad_low)
        + through_weight(value_w, values_grad_low)
    ).astype(jnp.bfloat16)
    summed = lax.psum(
        (
            grad_query_w,
            grad_key_w,
            grad_value_w,
            grad_query_b,
            grad_value_b,
            grad_weight,
            grad_output_b,
            grad_first_gain,
            grad_first_shift,
            grad_inner_w,
            grad_inner_b,
            grad_outer_w,
            grad_outer_b,
            grad_second_gain,
            grad_second_shift,
        ),
        "dp",
    )
    return (
        layer_out,
        input_grad,
        summed[0],
        summed[1],
        summed[2],
        summed[3],
        summed[4],
        summed[5],
        summed[6],
        summed[7],
        summed[8],
        summed[9],
        summed[10],
        summed[11],
        summed[12],
        summed[13],
        summed[14],
    )


def solution(mesh):
    placed = (
        P("tensor", "dp"),
        P("tensor", "dp"),
        P("tensor", None),
        P("tensor", None),
        P("tensor", None),
        P("tensor"),
        P("tensor"),
        P(None, "tensor"),
        P("tensor"),
        P("tensor"),
        P("tensor"),
        P("tensor", None),
        P("tensor"),
        P("tensor", None),
        P("tensor"),
        P("tensor"),
        P("tensor"),
    )
    return jax.shard_map(
        shards,
        mesh=mesh,
        in_specs=placed,
        out_specs=(
            P("tensor", "dp"),
            P("tensor", "dp"),
            P("tensor", None),
            P("tensor", None),
            P("tensor", None),
            P("tensor"),
            P("tensor"),
            P(None, "tensor"),
            P("tensor"),
            P("tensor"),
            P("tensor"),
            P("tensor", None),
            P("tensor"),
            P("tensor", None),
            P("tensor"),
            P("tensor"),
            P("tensor"),
        ),
        check_vma=False,
    )
```

profile of v0, /device:TPU:0, one launch (start us, length us, event | category | flops | bytes accessed | tf_op | source)
XLA Modules:
  0.0 835.8 jit_solution(991804344389069406)
XLA Ops:
  21.0 4.1 copy_bitcast_fusion.3
  25.3 53.0 %while.58 = (s32[]{:T(128)}, bf16[4,3,64,1024]{3,2,1,0:T(8,128)(2,1)S(1)}, f32[4,3,1,1024]{3,2,1,0:T(1,128)}, f32[4,3,1,1024]{3,2,1,0:T(1,128)}, bf16[4,3,64,102...) while((s32[]{:T(128)}, ...), condition=%wide.region_5.6_spmd, body=%wide.region_0.5_spmd.sunk | while | flops 416805888 | bytes 26757424 | solution.py:144
  27.9 8.6 %while.61 = (s32[]{:T(128)}, bf16[2,3,64,512]{3,2,1,0:T(8,128)(2,1)S(1)}, f32[2,3,1,512]{3,1,2,0:T(4,128)S(1)}, f32[2,3,1,512]{3,1,2,0:T(4,128)S(1)}, bf16[2,3,6...) while((s32[]{:T(128)}, ...), condition=%wide.region_4.4_spmd, body=%wide.region_1.3_spmd.sunk | while | flops 416805888 | bytes 20318312 | solution.py:61
  41.1 8.6 %while.61 = (s32[]{:T(128)}, bf16[2,3,64,512]{3,2,1,0:T(8,128)(2,1)S(1)}, f32[2,3,1,512]{3,1,2,0:T(4,128)S(1)}, f32[2,3,1,512]{3,1,2,0:T(4,128)S(1)}, bf16[2,3,6...) while((s32[]{:T(128)}, ...), condition=%wide.region_4.4_spmd, body=%wide.region_1.3_spmd.sunk | while | flops 416805888 | bytes 20318312 | solution.py:61
  54.3 8.6 %while.61 = (s32[]{:T(128)}, bf16[2,3,64,512]{3,2,1,0:T(8,128)(2,1)S(1)}, f32[2,3,1,512]{3,1,2,0:T(4,128)S(1)}, f32[2,3,1,512]{3,1,2,0:T(4,128)S(1)}, bf16[2,3,6...) while((s32[]{:T(128)}, ...), condition=%wide.region_4.4_spmd, body=%wide.region_1.3_spmd.sunk | while | flops 416805888 | bytes 20318312 | solution.py:61
  67.5 8.6 %while.61 = (s32[]{:T(128)}, bf16[2,3,64,512]{3,2,1,0:T(8,128)(2,1)S(1)}, f32[2,3,1,512]{3,1,2,0:T(4,128)S(1)}, f32[2,3,1,512]{3,1,2,0:T(4,128)S(1)}, bf16[2,3,6...) while((s32[]{:T(128)}, ...), condition=%wide.region_4.4_spmd, body=%wide.region_1.3_spmd.sunk | while | flops 416805888 | bytes 20318312 | solution.py:61
  81.3 6.3 convolution_bitcast_fusion
  87.6 12.7 %copy.101 = f32[768,4096]{1,0:T(8,128)} copy(f32[768,4096]{0,1:T(8,128)} %convolution_bitcast_fusion) | data formatting | bytes 25165824
  100.4 214.7 %reduce-scatter.4.cloned.1.call-done = f32[192,4096]{1,0:T(8,128)} async-done(((f32[768,4096]{1,0:T(8,128)}), f32[192,4096]{1,0:T(8,128)}) %reduce-scatter.4.cloned.1.call-update) | async-done | bytes 3145744 | tf_op jit(solution)/shard_map/reduce_scatter | solution.py:146
  318.1 18.6 %psum.161 = f32[4096]{0:T(1024)S(1)} all-reduce(f32[4096]{0:T(1024)S(1)} %get-tuple-element.431), channel_id=1, replica_groups=mesh['dp'=8,'tensor'=4] {'tensor'}, use_global_device_ids=true, to_apply=%region_8.9 | all-reduce | flops 4096 | bytes 32768 | tf_op jit(solution)/shard_map/psum | solution.py:153
  337.1 15.5 %psum.162 = f32[4096]{0:T(1024)S(1)} all-reduce(f32[4096]{0:T(1024)S(1)} %multiply_reduce_fusion.7), channel_id=1, replica_groups=mesh['dp'=8,'tensor'=4] {'tensor'}, use_global_device_ids=true, to_apply=%region_10.11 | all-reduce | flops 4096 | bytes 32768 | tf_op jit(solution)/shard_map/psum | solution.py:155
  352.7 31.2 %fusion.39 = (bf16[768,4096]{0,1:T(8,128)(2,1)S(1)}, f32[768,4096]{0,1:T(8,128)}, f32[4096,768]{1,0:T(8,128)}) fusion(f32[768]{0:T(1024)S(1)} %copy-done.53, bf16[768,192]{0,1:T(8,128)(2,1)S(1)} %copy-done, f32[192,4096]{1,0:T(8,128)S(1)} %get-tuple-element.432, f32[192]{0:T(256)S(1)} %copy-done.55, f32[192]{0:T(256)S(1)} %copy-done.38, ...), kind=kOutput, calls=%fused_computation.74 | convolution fusion | flops 1419509760 | bytes 34935296 | tf_op jit(solution)/shard_map/dot_general | solution.py:160
  388.0 16.4 %psum.163 = f32[4096]{0:T(1024)S(1)} all-reduce(f32[4096]{0:T(1024)S(1)} %get-tuple-element.447), channel_id=1, replica_groups=mesh['dp'=8,'tensor'=4] {'tensor'}, use_global_device_ids=true, to_apply=%region_12.13 | all-reduce | flops 4096 | bytes 32768 | tf_op jit(solution)/shard_map/psum | solution.py:168
  406.7 15.8 %psum.164 = f32[4096]{0:T(1024)S(1)} all-reduce(f32[4096]{0:T(1024)S(1)} %multiply_reduce_fusion.6), channel_id=1, replica_groups=mesh['dp'=8,'tensor'=4] {'tensor'}, use_global_device_ids=true, to_apply=%region_14.15 | all-reduce | flops 4096 | bytes 32768 | tf_op jit(solution)/shard_map/psum | solution.py:170
  422.5 5.6 multiply_reduce_fusion.2
  428.1 16.3 %all-reduce.3 = (bf16[4096]{0:T(1024)(128)(2,1)S(1)}, bf16[4096]{0:T(1024)(128)(2,1)S(1)}) all-reduce(bf16[4096]{0:T(1024)(128)(2,1)S(1)} %get-tuple-element.331, bf16[4096]{0:T(1024)(128)(2,1)S(1)} %get-tuple-element.335), channel_id=1, replica_groups=mesh['dp'=8,'tensor'=4] {'tensor'}, use_global_device_ids=true, to_apply=%region_18.19 | all-reduce | flops 8192 | bytes 32768 | tf_op jit(solution)/shard_map/psum | solution.py:179
  444.5 6.1 convert_reduce_fusion.1
  450.6 13.0 %convert_reduce_fusion = (f32[768]{0:T(1024)}, bf16[768,4096]{0,1:T(8,128)(2,1)S(1)}) fusion(f32[768,4096]{0,1:T(8,128)} %get-tuple-element.430, bf16[192,768]{1,0:T(8,128)(2,1)S(1)} %copy-done.52, f32[192,4096]{1,0:T(8,128)S(1)} %get-tuple-element.426, f32[4096,768]{1,0:T(8,128)} %get-tuple-element.446, f32[768]{0:T(1024)S(1)} %copy-done.53), kind=kOutput, calls=%fused_computation.75 | convolution fusion | flops 1262222592 | bytes 34904064 | tf_op jit(solution)/shard_map/dot_general | solution.py:21
  463.6 4.6 multiply_reduce_fusion.3
  468.2 15.6 %all-reduce.2 = (bf16[4096]{0:T(1024)(128)(2,1)S(1)}, bf16[4096]{0:T(1024)(128)(2,1)S(1)}) all-reduce(bf16[4096]{0:T(1024)(128)(2,1)S(1)} %get-tuple-element.333, bf16[4096]{0:T(1024)(128)(2,1)S(1)} %get-tuple-element.334), channel_id=1, replica_groups=mesh['dp'=8,'tensor'=4] {'tensor'}, use_global_device_ids=true, to_apply=%region_22.23 | all-reduce | flops 8192 | bytes 32768 | tf_op jit(solution)/shard_map/psum | solution.py:199
  483.8 4.9 convert_reduce_fusion.2
  489.1 6.0 fusion.63
  495.1 5.7 fusion.67
  500.8 102.0 %all-gather.2.cloned.1.call-done = bf16[768,4096]{1,0:T(8,128)(2,1)} async-done(((bf16[192,4096]{1,0:T(8,128)(2,1)}), bf16[768,4096]{1,0:T(8,128)(2,1)}) %all-gather.2.cloned.1.call-update) | async-done | bytes 6291472 | tf_op jit(solution)/shard_map/all_gather | solution.py:208
  602.8 4.2 fusion.61
  613.9 121.6 %while.60 = (s32[]{:T(128)}, bf16[4,3,64,1024]{3,2,1,0:T(8,128)(2,1)}, bf16[4,3,64,1024]{3,2,1,0:T(8,128)(2,1)}, bf16[4,3,64,1024]{3,2,1,0:T(8,128)(2,1)}, bf16[...) while((s32[]{:T(128)}, ...), condition=%wide.region_27.28_spmd, body=%wide.region_23.27_spmd.sunk | while | flops 1021868544 | bytes 70955544 | solution.py:216
  622.5 18.3 %while.62 = (s32[]{:T(128)}, f32[3,64,1024]{2,1,0:T(8,128)S(1)}, f32[3,64,1024]{2,1,0:T(8,128)S(1)}, bf16[2,3,64,512]{3,2,1,0:T(8,128)(2,1)}, bf16[2,3,64,512]{3...) while((s32[]{:T(128)}, f32[3,64,1024]{2,1,0:T(8,128)S(1)}, ...), condition=%wide.region_26.26_spmd.clone, body=%wide.region_24.25_spmd.clone.sunk | while | flops 1021868544 | bytes 59060492 | solution.py:99
  652.9 18.3 %while.62 = (s32[]{:T(128)}, f32[3,64,1024]{2,1,0:T(8,128)S(1)}, f32[3,64,1024]{2,1,0:T(8,128)S(1)}, bf16[2,3,64,512]{3,2,1,0:T(8,128)(2,1)}, bf16[2,3,64,512]{3...) while((s32[]{:T(128)}, f32[3,64,1024]{2,1,0:T(8,128)S(1)}, ...), condition=%wide.region_26.26_spmd.clone, body=%wide.region_24.25_spmd.clone.sunk | while | flops 1021868544 | bytes 59060492 | solution.py:99
  683.3 18.3 %while.62 = (s32[]{:T(128)}, f32[3,64,1024]{2,1,0:T(8,128)S(1)}, f32[3,64,1024]{2,1,0:T(8,128)S(1)}, bf16[2,3,64,512]{3,2,1,0:T(8,128)(2,1)}, bf16[2,3,64,512]{3...) while((s32[]{:T(128)}, f32[3,64,1024]{2,1,0:T(8,128)S(1)}, ...), condition=%wide.region_26.26_spmd.clone, body=%wide.region_24.25_spmd.clone.sunk | while | flops 1021868544 | bytes 59060492 | solution.py:99
  713.6 18.3 %while.62 = (s32[]{:T(128)}, f32[3,64,1024]{2,1,0:T(8,128)S(1)}, f32[3,64,1024]{2,1,0:T(8,128)S(1)}, bf16[2,3,64,512]{3,2,1,0:T(8,128)(2,1)}, bf16[2,3,64,512]{3...) while((s32[]{:T(128)}, f32[3,64,1024]{2,1,0:T(8,128)S(1)}, ...), condition=%wide.region_26.26_spmd.clone, body=%wide.region_24.25_spmd.clone.sunk | while | flops 1021868544 | bytes 59060492 | solution.py:99
  757.0 25.1 %all-reduce = (f32[192]{0:T(256)}, f32[192]{0:T(256)}, f32[192]{0:T(256)}, f32[192]{0:T(256)}, f32[192]{0:T(256)}, /*index=5*/f32[768]{0:T(1024)}, f32[192]{0:T(256)}, f32[192]{0:T(256)}, f32[192]{0:T(256)}) all-reduce(f32[192]{0:T(256)S(1)} %reduce_sum.184, f32[192]{0:T(256)S(1)} %reduce_sum.186, ...), channel_id=1, replica_groups=mesh['dp'=8,'tensor'=4] {'dp'}, use_global_device_ids=true, to_apply=%region_32.33 | all-reduce | flops 2304 | bytes 18432 | tf_op jit(solution)/shard_map/psum | solution.py:233
  789.0 30.4 %all-reduce.6.cloned.1.call-done = (f32[192,192]{1,0:T(8,128)}, f32[192,192]{1,0:T(8,128)}, f32[192,192]{1,0:T(8,128)}, f32[768,192]{0,1:T(8,128)}, f32[768,192]{0,1:T(8,128)}, /*index=5*/f32[192,768]{1,0:T(8,128)}) async-done(((f32[192,192]{1,0:T(8,128)}, f32[192,192]{1,0:T(8,128)}, f32[192,192]{1,0:T(8,128)}, f32[768,192]{0,1:T(8,128)}, f32[768,192]{0,1:T(8,128)}, /*index=5*/f32[192,768]{1,0:T(8,128)}), ...) | async-done | bytes 2211856 | tf_op jit(solution)/shard_map/psum | solution.py:233
  (477 shorter events, 244.0 us)
Async XLA Ops:
  7.2 345.5 %copy-start = (bf16[768,192]{0,1:T(8,128)(2,1)S(1)}, bf16[768,192]{0,1:T(8,128)(2,1)}, u32[]{:S(2)}) copy-start(bf16[768,192]{0,1:T(8,128)(2,1)} %param.36) | copy-start | bytes 884740
  7.2 307.9 %reduce-scatter.4.cloned.1.call-start = ((), (), s32[]{:S(2)}) async-start(), calls=%async_computation.2 | async-start | bytes 15728640 | tf_op jit(solution)/shard_map/reduce_scatter | solution.py:146
  10.4 4.6 copy-start.48
  100.3 214.8 %copy-start.49 = (f32[192]{0:T(256)S(1)}, f32[192]{0:T(256)}, u32[]{:S(2)}) copy-start(f32[192]{0:T(256)} %param.33) | copy-start | bytes 2308
  100.4 502.5 %all-gather.2.cloned.1.call-start = ((), (), s32[]{:S(2)}) async-start(), calls=%async_computation.1 | async-start | bytes 7864320 | tf_op jit(solution)/shard_map/all_gather | solution.py:208
  318.0 177.1 %copy-start.4 = (f32[192,4096]{1,0:T(8,128)}, f32[192,4096]{1,0:T(8,128)S(1)}, u32[]{:S(2)}) copy-start(f32[192,4096]{1,0:T(8,128)S(1)} %get-tuple-element.432) | copy-start | bytes 9437188
  318.0 34.6 %copy-start.38 = (f32[192]{0:T(256)S(1)}, f32[192]{0:T(256)}, u32[]{:S(2)}) copy-start(f32[192]{0:T(256)} %param.34) | copy-start | bytes 2308
  318.1 34.6 %copy-start.53 = (f32[768]{0:T(1024)S(1)}, f32[768]{0:T(1024)}, u32[]{:S(2)}) copy-start(f32[768]{0:T(1024)} %param.37) | copy-start | bytes 9220
  318.1 34.6 %copy-start.55 = (f32[192]{0:T(256)S(1)}, f32[192]{0:T(256)}, u32[]{:S(2)}) copy-start(f32[192]{0:T(256)} %param.35) | copy-start | bytes 2308
  336.7 158.4 %copy-start.22 = (f32[4096]{0:T(1024)}, f32[4096]{0:T(1024)S(1)}, u32[]{:S(2)}) copy-start(f32[4096]{0:T(1024)S(1)} %broadcast_multiply_fusion.1) | copy-start | bytes 49156
  352.7 142.4 %copy-start.25 = (f32[4096]{0:T(1024)}, f32[4096]{0:T(1024)S(1)}, u32[]{:S(2)}) copy-start(f32[4096]{0:T(1024)S(1)} %add_rsqrt_fusion.1) | copy-start | bytes 49156
  352.7 31.3 %copy-start.51 = (bf16[192,768]{1,0:T(8,128)(2,1)S(1)}, bf16[192,768]{1,0:T(8,128)(2,1)}, u32[]{:S(2)}) copy-start(bf16[192,768]{1,0:T(8,128)(2,1)} %param.38) | copy-start | bytes 884740
  352.7 31.3 %copy-start.54 = (f32[192]{0:T(256)S(1)}, f32[192]{0:T(256)}, u32[]{:S(2)}) copy-start(f32[192]{0:T(256)} %param.39) | copy-start | bytes 2308
  388.0 34.5 %copy-start.40 = (f32[192]{0:T(256)S(1)}, f32[192]{0:T(256)}, u32[]{:S(2)}) copy-start(f32[192]{0:T(256)} %param.40) | copy-start | bytes 2308
  422.5 22.0 %copy-start.50 = (f32[192]{0:T(256)S(1)}, f32[192]{0:T(256)}, u32[]{:S(2)}) copy-start(f32[192]{0:T(256)} %param.41) | copy-start | bytes 2308
  444.5 6.1 copy-start.52
  450.5 13.0 %copy-start.8 = (f32[192,4096]{1,0:T(8,128)}, f32[192,4096]{1,0:T(8,128)S(1)}, u32[]{:S(2)}) copy-start(f32[192,4096]{1,0:T(8,128)S(1)} %get-tuple-element.426) | copy-start | bytes 9437188
  483.7 4.9 copy-start.34
  483.7 4.9 copy-start.36
  488.7 330.8 %all-reduce.6.cloned.1.call-start = ((), (), s32[]{:S(2)}) async-start(), calls=%async_computation.3 | async-start | bytes 4718592 | tf_op jit(solution)/shard_map/psum | solution.py:233
  489.1 6.0 copy-start.56
  495.1 107.7 %copy-start.33 = (bf16[768,192]{0,1:T(8,128)(2,1)S(1)}, bf16[768,192]{0,1:T(8,128)(2,1)}, u32[]{:S(2)}) copy-start(bf16[768,192]{0,1:T(8,128)(2,1)} %param.32) | copy-start | bytes 884740
  746.3 7.3 slice-start
  753.7 28.3 %copy-start.5 = (f32[192,4096]{1,0:T(8,128)S(1)}, f32[192,4096]{1,0:T(8,128)}, u32[]{:S(2)}) copy-start(f32[192,4096]{1,0:T(8,128)} %copy-done.4) | copy-start | bytes 9437188
  753.7 28.3 %copy-start.23 = (f32[4096]{0:T(1024)S(1)}, f32[4096]{0:T(1024)}, u32[]{:S(2)}) copy-start(f32[4096]{0:T(1024)} %copy-done.22) | copy-start | bytes 49156
  753.8 28.3 %copy-start.26 = (f32[4096]{0:T(1024)S(1)}, f32[4096]{0:T(1024)}, u32[]{:S(2)}) copy-start(f32[4096]{0:T(1024)} %copy-done.25) | copy-start | bytes 49156
  753.8 28.3 %copy-start.27 = (bf16[192,192]{1,0:T(8,128)(2,1)S(1)}, bf16[192,192]{1,0:T(8,128)(2,1)}, u32[]{:S(2)}) copy-start(bf16[192,192]{1,0:T(8,128)(2,1)} %param.27) | copy-start | bytes 221188
  753.8 28.3 %copy-start.35 = (f32[4096]{0:T(1024)S(1)}, f32[4096]{0:T(1024)}, u32[]{:S(2)}) copy-start(f32[4096]{0:T(1024)} %copy-done.34) | copy-start | bytes 49156
  753.8 28.3 %copy-start.37 = (f32[4096]{0:T(1024)S(1)}, f32[4096]{0:T(1024)}, u32[]{:S(2)}) copy-start(f32[4096]{0:T(1024)} %copy-done.36) | copy-start | bytes 49156
  753.8 28.3 %copy-start.39 = (f32[192]{0:T(256)S(1)}, f32[192]{0:T(256)}, u32[]{:S(2)}) copy-start(f32[192]{0:T(256)} %param.34) | copy-start | bytes 2308
  787.2 41.8 %copy-start.1 = (bf16[768,192]{0,1:T(8,128)(2,1)S(1)}, bf16[768,192]{0,1:T(8,128)(2,1)}, u32[]{:S(2)}) copy-start(bf16[768,192]{0,1:T(8,128)(2,1)} %param.36) | copy-start | bytes 884740
  819.5 8.7 %copy-start.24 = (f32[192,768]{1,0:T(8,128)S(1)}, f32[192,768]{1,0:T(8,128)}, u32[]{:S(2)}) copy-start(f32[192,768]{1,0:T(8,128)} %get-tuple-element.879) | copy-start | bytes 1769476
  (58 other events, 124.6 us)
Sparse Core Ops, SparseCore 0:
  100.5 214.6 reduce-scatter.3
  488.8 113.9 all-gather.1
  757.0 62.4 all-reduce.5
where the time goes:
time: 845 us; the launch traced here: 836 us
  waiting for transfers between devices  347 us (41%)
  matrix products  184 us (22%)
  local copies, waits for them, and re-layouts  124 us (15%)
  blocking collectives  123 us (15%)
  other arithmetic  39.5 us (5%)
  between operations  14.7 us (2%)
    reduce_scatter x1, waiting for transfers between devices, shards(): lax.psum_scatter(jnp.dot(output_w, context_low, preferred_element_type=jn...  215 us
    all_gather x1, waiting for transfers between devices, shards(): piece = lax.all_gather(attended_grad_low, 'tensor', axis=0, tiled=True)  102 us
    dot_general x1, matrix products, shards(): jnp.dot(inner_w, hidden_low, preferred_element_type=jnp.float32)  31.2 us
    psum x1, waiting for transfers between devices, shards(): lax.psum((grad_query_w, grad_key_w, grad_value_w, grad_query_b, grad_valu...  30.4 us
    unnamed x121, local copies, waits for them, and re-layouts  30.3 us
    dot_general x16, matrix products, one_block(): jnp.einsum('hdq,hdk->hqk', query_part, keys, preferred_element_type=jnp.f...  30 us
    dot_general x6, matrix products, through_weight(): lax.dot_general(weight, grad, (((0,), (0,)), ((), ())), preferred_element...  27.8 us
    psum x1, blocking collectives, shards(): lax.psum((grad_query_w, grad_key_w, grad_value_w, grad_query_b, grad_valu...  25.1 us
  transfers between devices with their start and end apart: 3, of which 3 were waited for; matrix products, arithmetic and copies ran while one was open for 2% of the time, Pallas kernels for 0%

commit v1 on v0

--- a/solution.py
+++ b/solution.py
@@ -205,7 +205,38 @@
     )
     attended_grad_low = grad_first_resid.astype(jnp.bfloat16)
     grad_output_b = jnp.sum(attended_grad_low.astype(jnp.float32), axis=1)
-    piece = lax.all_gather(attended_grad_low, "tensor", axis=0, tiled=True)
+    kept_rows = []
+    piece_now, o_now, u1 = (
+        lax.axis_size("tensor"),
+        lax.axis_index("tensor"),
+        attended_grad_low.shape[0],
+    )
+    d = 0
+    while d < piece_now:
+        kept_rows.append((d, (d + 1) % piece_now))
+        d += 1
+    frames = []
+    d = 0
+    while d < piece_now:
+        frames.append((d, (d - 1) % piece_now))
+        d = d + 1
+    piece = jnp.zeros(
+        (*attended_grad_low.shape[:0], piece_now * u1, *attended_grad_low.shape[0 + 1 :]),
+        attended_grad_low.dtype,
+    )
+    extra = h_now = attended_grad_low
+    piece = lax.dynamic_update_slice_in_dim(piece, attended_grad_low, o_now * u1, axis=0)
+    value_now = piece_now // 2
+    j = 1
+    while j < value_now + 1:
+        extra = lax.ppermute(extra, "tensor", perm=kept_rows)
+        piece = lax.dynamic_update_slice_in_dim(piece, extra, (o_now - j) % piece_now * u1, axis=0)
+        if j < piece_now - value_now:
+            h_now = lax.ppermute(h_now, "tensor", frames)
+            piece = lax.dynamic_update_slice_in_dim(
+                piece, h_now, (o_now + j) % piece_now * u1, axis=0
+            )
+        j = j + 1
     start = jnp.int32(0)
     weight_rows = lax.dynamic_slice_in_dim(output_w, start, piece.shape[0], 0)
     grad_ctx = jnp.zeros((local, tokens), jnp.float32) + through_weight(weight_rows, piece)

time: 845 us -> 853 us (level)
  waiting for transfers between devices: 347 us -> 287 us
  matrix products: 184 us -> 208 us
  blocking collectives: 123 us -> 146 us
  local copies, waits for them, and re-layouts: 124 us -> 140 us
    all_gather x1 -> x0, waiting for transfers between devices: 102 us -> none  [shards(): piece = lax.all_gather(attended_grad_low, 'tensor', axis=0, tiled=True)]
    ppermute x0 -> x3, waiting for transfers between devices: none -> 39.1 us  [the longest x2 32.6 us: shards(): extra = lax.ppermute(extra, 'tensor', perm=kept_rows)]
    psum x1, blocking collectives: 15.6 us -> 41 us  [shards(): lax.psum(jnp.sum(first_scaled * first_normed, axis=0).astype(jnp.bfloat16...]
    dot_general x8, matrix products: 5.85 us -> 22.3 us  [one_block(): jnp.einsum('hqk,hdq->hdk', grad_scores, query_part, preferred_element_typ...]
    while x72 -> x192, local copies, waits for them, and re-layouts: 6.6 us -> 22 us
    dot_general x8, matrix products: 8.64 us -> 21.9 us  [one_block(): jnp.einsum('hqk,hdk->hdq', grad_scores, keys, preferred_element_type=jnp....]
    dot_general x8, matrix products: 17.3 us -> 8.19 us  [one_block(): jnp.einsum('hdq,hdk->hqk', grad_part, values, preferred_element_type=jnp....]
    dynamic_update_slice x20, local copies, waits for them, and re-layouts: 12.2 us -> 21.2 us  [shards(): lax.map(attend_forward, (query_seq, keys_seq, values_seq))]
  transfers between devices with their start and end apart: 3 -> 5, of which waited for: 3 -> 5; matrix products, arithmetic and copies ran while one was open for 2% -> 2% of each run, Pallas kernels for 0% -> 0%
where the time goes in v1:
time: 853 us; the launch traced here: 844 us
  waiting for transfers between devices  287 us (34%)
  matrix products  208 us (24%)
  blocking collectives  146 us (17%)
  local copies, waits for them, and re-layouts  140 us (16%)
  other arithmetic  41 us (5%)
  between operations  15 us (2%)
    reduce_scatter x1, waiting for transfers between devices, shards(): lax.psum_scatter(jnp.dot(output_w, context_low, preferred_element_type=jn...  215 us
    psum x1, blocking collectives, shards(): lax.psum(jnp.sum(first_scaled * first_normed, axis=0).astype(jnp.bfloat16...  41 us
    psum x1, waiting for transfers between devices, shards(): lax.psum((grad_query_w, grad_key_w, grad_value_w, grad_query_b, grad_valu...  33 us
    ppermute x2, waiting for transfers between devices, shards(): extra = lax.ppermute(extra, 'tensor', perm=kept_rows)  32.6 us
    dot_general x1, matrix products, shards(): jnp.dot(inner_w, hidden_low, preferred_element_type=jnp.float32)  31.3 us
    unnamed x123, local copies, waits for them, and re-layouts  30.8 us
    dot_general x16, matrix products, one_block(): jnp.einsum('hdq,hdk->hqk', query_part, keys, preferred_element_type=jnp.f...  30 us
    dot_general x6, matrix products, through_weight(): lax.dot_general(weight, grad, (((0,), (0,)), ((), ())), preferred_element...  25.2 us
  transfers between devices with their start and end apart: 5, of which 5 were waited for; matrix products, arithmetic and copies ran while one was open for 2% of the time, Pallas kernels for 0%

profile of v1, /device:TPU:0, one launch (start us, length us, event | category | flops | bytes accessed | tf_op | source)
XLA Modules:
  0.0 844.5 jit_solution(2810689557432233469)
XLA Ops:
  26.4 51.9 %while.58 = (s32[]{:T(128)}, bf16[4,3,64,1024]{3,2,1,0:T(8,128)(2,1)}, f32[4,3,1,1024]{3,2,1,0:T(1,128)}, f32[4,3,1,1024]{3,2,1,0:T(1,128)}, bf16[4,3,64,1024]{3...) while((s32[]{:T(128)}, ...), condition=%wide.region_5.6_spmd, body=%wide.region_0.5_spmd.sunk | while | flops 416805888 | bytes 26758932 | solution.py:144
  28.0 8.6 %while.61 = (s32[]{:T(128)}, bf16[2,3,64,512]{3,2,1,0:T(8,128)(2,1)S(1)}, f32[2,3,1,512]{3,1,2,0:T(4,128)S(1)}, f32[2,3,1,512]{3,1,2,0:T(4,128)S(1)}, bf16[2,3,6...) while((s32[]{:T(128)}, ...), condition=%wide.region_4.4_spmd, body=%wide.region_1.3_spmd.sunk | while | flops 416805888 | bytes 20318304 | solution.py:61
  40.9 8.6 %while.61 = (s32[]{:T(128)}, bf16[2,3,64,512]{3,2,1,0:T(8,128)(2,1)S(1)}, f32[2,3,1,512]{3,1,2,0:T(4,128)S(1)}, f32[2,3,1,512]{3,1,2,0:T(4,128)S(1)}, bf16[2,3,6...) while((s32[]{:T(128)}, ...), condition=%wide.region_4.4_spmd, body=%wide.region_1.3_spmd.sunk | while | flops 416805888 | bytes 20318304 | solution.py:61
  53.8 8.6 %while.61 = (s32[]{:T(128)}, bf16[2,3,64,512]{3,2,1,0:T(8,128)(2,1)S(1)}, f32[2,3,1,512]{3,1,2,0:T(4,128)S(1)}, f32[2,3,1,512]{3,1,2,0:T(4,128)S(1)}, bf16[2,3,6...) while((s32[]{:T(128)}, ...), condition=%wide.region_4.4_spmd, body=%wide.region_1.3_spmd.sunk | while | flops 416805888 | bytes 20318304 | solution.py:61
  66.8 8.6 %while.61 = (s32[]{:T(128)}, bf16[2,3,64,512]{3,2,1,0:T(8,128)(2,1)S(1)}, f32[2,3,1,512]{3,1,2,0:T(4,128)S(1)}, f32[2,3,1,512]{3,1,2,0:T(4,128)S(1)}, bf16[2,3,6...) while((s32[]{:T(128)}, ...), condition=%wide.region_4.4_spmd, body=%wide.region_1.3_spmd.sunk | while | flops 416805888 | bytes 20318304 | solution.py:61
  83.3 6.3 convolution_bitcast_fusion
  89.7 12.7 %copy.101 = f32[768,4096]{1,0:T(8,128)} copy(f32[768,4096]{0,1:T(8,128)} %convolution_bitcast_fusion) | data formatting | bytes 25165824
  102.4 214.7 %reduce-scatter.4.cloned.1.call-done = f32[192,4096]{1,0:T(8,128)} async-done(((f32[768,4096]{1,0:T(8,128)}), f32[192,4096]{1,0:T(8,128)}) %reduce-scatter.4.cloned.1.call-update) | async-done | bytes 3145744 | tf_op jit(solution)/shard_map/reduce_scatter | solution.py:146
  320.1 18.6 %psum.161 = f32[4096]{0:T(1024)S(1)} all-reduce(f32[4096]{0:T(1024)S(1)} %get-tuple-element.431), channel_id=1, replica_groups=mesh['dp'=8,'tensor'=4] {'tensor'}, use_global_device_ids=true, to_apply=%region_8.9 | all-reduce | flops 4096 | bytes 32768 | tf_op jit(solution)/shard_map/psum | solution.py:153
  339.1 15.5 %psum.162 = f32[4096]{0:T(1024)S(1)} all-reduce(f32[4096]{0:T(1024)S(1)} %multiply_reduce_fusion.7), channel_id=1, replica_groups=mesh['dp'=8,'tensor'=4] {'tensor'}, use_global_device_ids=true, to_apply=%region_10.11 | all-reduce | flops 4096 | bytes 32768 | tf_op jit(solution)/shard_map/psum | solution.py:155
  354.7 31.3 %fusion.39 = (bf16[768,4096]{0,1:T(8,128)(2,1)S(1)}, f32[768,4096]{0,1:T(8,128)}, f32[4096,768]{1,0:T(8,128)}) fusion(f32[768]{0:T(1024)S(1)} %copy-done.65, bf16[768,192]{0,1:T(8,128)(2,1)S(1)} %copy-done, f32[192,4096]{1,0:T(8,128)S(1)} %get-tuple-element.432, f32[192]{0:T(256)S(1)} %copy-done.67, f32[192]{0:T(256)S(1)} %copy-done.49, ...), kind=kOutput, calls=%fused_computation.74 | convolution fusion | flops 1419509760 | bytes 34935296 | tf_op jit(solution)/shard_map/dot_general | solution.py:160
  390.1 16.4 %psum.163 = f32[4096]{0:T(1024)S(1)} all-reduce(f32[4096]{0:T(1024)S(1)} %get-tuple-element.447), channel_id=1, replica_groups=mesh['dp'=8,'tensor'=4] {'tensor'}, use_global_device_ids=true, to_apply=%region_12.13 | all-reduce | flops 4096 | bytes 32768 | tf_op jit(solution)/shard_map/psum | solution.py:168
  408.8 15.8 %psum.164 = f32[4096]{0:T(1024)S(1)} all-reduce(f32[4096]{0:T(1024)S(1)} %multiply_reduce_fusion.6), channel_id=1, replica_groups=mesh['dp'=8,'tensor'=4] {'tensor'}, use_global_device_ids=true, to_apply=%region_14.15 | all-reduce | flops 4096 | bytes 32768 | tf_op jit(solution)/shard_map/psum | solution.py:170
  424.6 5.6 multiply_reduce_fusion.2
  430.2 16.3 %all-reduce.3 = (bf16[4096]{0:T(1024)(128)(2,1)S(1)}, bf16[4096]{0:T(1024)(128)(2,1)S(1)}) all-reduce(bf16[4096]{0:T(1024)(128)(2,1)S(1)} %get-tuple-element.331, bf16[4096]{0:T(1024)(128)(2,1)S(1)} %get-tuple-element.335), channel_id=1, replica_groups=mesh['dp'=8,'tensor'=4] {'tensor'}, use_global_device_ids=true, to_apply=%region_18.19 | all-reduce | flops 8192 | bytes 32768 | tf_op jit(solution)/shard_map/psum | solution.py:179
  446.6 6.1 convert_reduce_fusion.1
  452.7 13.0 %convert_reduce_fusion = (f32[768]{0:T(1024)}, bf16[768,4096]{0,1:T(8,128)(2,1)S(1)}) fusion(f32[768,4096]{0,1:T(8,128)} %get-tuple-element.430, bf16[192,768]{1,0:T(8,128)(2,1)S(1)} %copy-done.64, f32[192,4096]{1,0:T(8,128)S(1)} %get-tuple-element.426, f32[4096,768]{1,0:T(8,128)} %get-tuple-element.446, f32[768]{0:T(1024)S(1)} %copy-done.65), kind=kOutput, calls=%fused_computation.75 | convolution fusion | flops 1262222592 | bytes 34904064 | tf_op jit(solution)/shard_map/dot_general | solution.py:21
  465.7 4.6 multiply_reduce_fusion.3
  470.3 41.0 %all-reduce.2 = (bf16[4096]{0:T(1024)(128)(2,1)S(1)}, bf16[4096]{0:T(1024)(128)(2,1)S(1)}) all-reduce(bf16[4096]{0:T(1024)(128)(2,1)S(1)} %get-tuple-element.333, bf16[4096]{0:T(1024)(128)(2,1)S(1)} %get-tuple-element.334), channel_id=1, replica_groups=mesh['dp'=8,'tensor'=4] {'tensor'}, use_global_device_ids=true, to_apply=%region_22.23 | all-reduce | flops 8192 | bytes 32768 | tf_op jit(solution)/shard_map/psum | solution.py:199
  511.3 4.8 convert_reduce_fusion.2
  520.0 5.1 fusion.67
  525.1 16.0 %collective-permute-done = bf16[192,4096]{1,0:T(8,128)(2,1)} collective-permute-done((bf16[192,4096]{1,0:T(8,128)(2,1)}, bf16[192,4096]{1,0:T(8,128)(2,1)}, u32[]{:S(2)}, u32[]{:S(2)}) %collective-permute-start) | collective-permute-done | bytes 1572896 | tf_op jit(solution)/shard_map/ppermute | solution.py:232
  544.6 5.0 fusion.63
  551.3 6.5 collective-permute-done.1
  557.9 16.7 %collective-permute-done.2 = bf16[192,4096]{1,0:T(8,128)(2,1)S(1)} collective-permute-done((bf16[192,4096]{1,0:T(8,128)(2,1)}, bf16[192,4096]{1,0:T(8,128)(2,1)S(1)}, u32[]{:S(2)}, u32[]{:S(2)}) %collective-permute-start.2) | collective-permute-done | bytes 1572896 | tf_op jit(solution)/shard_map/ppermute | solution.py:232
  585.1 163.0 %while.60 = (s32[]{:T(128)}, bf16[4,3,64,1024]{3,2,1,0:T(8,128)(2,1)}, bf16[4,3,64,1024]{3,2,1,0:T(8,128)(2,1)}, bf16[4,3,64,1024]{3,2,1,0:T(8,128)(2,1)}, bf16[...) while((s32[]{:T(128)}, ...), condition=%wide.region_27.28_spmd, body=%wide.region_23.27_spmd.sunk | while | flops 1021868544 | bytes 141737248 | solution.py:247
  590.7 31.0 %while.62 = (s32[]{:T(128)}, f32[3,64,1024]{2,1,0:T(8,128)}, f32[3,64,1024]{2,1,0:T(8,128)}, bf16[2,3,64,512]{3,2,1,0:T(8,128)(2,1)}, bf16[2,3,64,512]{3,2,1,0:T...) while((s32[]{:T(128)}, f32[3,64,1024]{2,1,0:T(8,128)}, ...), condition=%wide.region_26.26_spmd.clone, body=%wide.region_24.25_spmd.clone.sunk | while | flops 1021868544 | bytes 115685312 | solution.py:99
  631.4 31.0 %while.62 = (s32[]{:T(128)}, f32[3,64,1024]{2,1,0:T(8,128)}, f32[3,64,1024]{2,1,0:T(8,128)}, bf16[2,3,64,512]{3,2,1,0:T(8,128)(2,1)}, bf16[2,3,64,512]{3,2,1,0:T...) while((s32[]{:T(128)}, f32[3,64,1024]{2,1,0:T(8,128)}, ...), condition=%wide.region_26.26_spmd.clone, body=%wide.region_24.25_spmd.clone.sunk | while | flops 1021868544 | bytes 115685312 | solution.py:99
  672.1 31.0 %while.62 = (s32[]{:T(128)}, f32[3,64,1024]{2,1,0:T(8,128)}, f32[3,64,1024]{2,1,0:T(8,128)}, bf16[2,3,64,512]{3,2,1,0:T(8,128)(2,1)}, bf16[2,3,64,512]{3,2,1,0:T...) while((s32[]{:T(128)}, f32[3,64,1024]{2,1,0:T(8,128)}, ...), condition=%wide.region_26.26_spmd.clone, body=%wide.region_24.25_spmd.clone.sunk | while | flops 1021868544 | bytes 115685312 | solution.py:99
  712.8 31.0 %while.62 = (s32[]{:T(128)}, f32[3,64,1024]{2,1,0:T(8,128)}, f32[3,64,1024]{2,1,0:T(8,128)}, bf16[2,3,64,512]{3,2,1,0:T(8,128)(2,1)}, bf16[2,3,64,512]{3,2,1,0:T...) while((s32[]{:T(128)}, f32[3,64,1024]{2,1,0:T(8,128)}, ...), condition=%wide.region_26.26_spmd.clone, body=%wide.region_24.25_spmd.clone.sunk | while | flops 1021868544 | bytes 115685312 | solution.py:99
  765.2 22.7 %all-reduce = (f32[192]{0:T(256)}, f32[192]{0:T(256)}, f32[192]{0:T(256)}, f32[192]{0:T(256)}, f32[192]{0:T(256)}, /*index=5*/f32[768]{0:T(1024)}, f32[192]{0:T(256)}, f32[192]{0:T(256)}, f32[192]{0:T(256)}) all-reduce(f32[192]{0:T(256)S(1)} %reduce_sum.184, f32[192]{0:T(256)S(1)} %reduce_sum.186, ...), channel_id=1, replica_groups=mesh['dp'=8,'tensor'=4] {'dp'}, use_global_device_ids=true, to_apply=%region_32.33 | all-reduce | flops 2304 | bytes 18432 | tf_op jit(solution)/shard_map/psum | solution.py:264
  794.9 33.0 %all-reduce.6.cloned.1.call-done = (f32[192,192]{1,0:T(8,128)}, f32[192,192]{1,0:T(8,128)}, f32[192,192]{1,0:T(8,128)}, f32[768,192]{0,1:T(8,128)}, f32[768,192]{0,1:T(8,128)}, /*index=5*/f32[192,768]{1,0:T(8,128)}) async-done(((f32[192,192]{1,0:T(8,128)}, f32[192,192]{1,0:T(8,128)}, f32[192,192]{1,0:T(8,128)}, f32[768,192]{0,1:T(8,128)}, f32[768,192]{0,1:T(8,128)}, /*index=5*/f32[192,768]{1,0:T(8,128)}), ...) | async-done | bytes 2211856 | tf_op jit(solution)/shard_map/psum | solution.py:264
  (606 shorter events, 299.0 us)
Async XLA Ops:
  7.2 347.5 %copy-start = (bf16[768,192]{0,1:T(8,128)(2,1)S(1)}, bf16[768,192]{0,1:T(8,128)(2,1)}, u32[]{:S(2)}) copy-start(bf16[768,192]{0,1:T(8,128)(2,1)} %param.36) | copy-start | bytes 884740
  7.2 310.0 %reduce-scatter.4.cloned.1.call-start = ((), (), s32[]{:S(2)}) async-start(), calls=%async_computation.1 | async-start | bytes 15728640 | tf_op jit(solution)/shard_map/reduce_scatter | solution.py:146
  102.4 214.8 %copy-start.61 = (f32[192]{0:T(256)S(1)}, f32[192]{0:T(256)}, u32[]{:S(2)}) copy-start(f32[192]{0:T(256)} %param.33) | copy-start | bytes 2308
  102.4 725.5 %all-reduce.6.cloned.1.call-start = ((), (), s32[]{:S(2)}) async-start(), calls=%async_computation.2 | async-start | bytes 4718592 | tf_op jit(solution)/shard_map/psum | solution.py:264
  320.1 199.9 %copy-start.12 = (f32[192,4096]{1,0:T(8,128)}, f32[192,4096]{1,0:T(8,128)S(1)}, u32[]{:S(2)}) copy-start(f32[192,4096]{1,0:T(8,128)S(1)} %get-tuple-element.432) | copy-start | bytes 9437188
  320.1 34.6 %copy-start.49 = (f32[192]{0:T(256)S(1)}, f32[192]{0:T(256)}, u32[]{:S(2)}) copy-start(f32[192]{0:T(256)} %param.34) | copy-start | bytes 2308
  320.1 34.6 %copy-start.65 = (f32[768]{0:T(1024)S(1)}, f32[768]{0:T(1024)}, u32[]{:S(2)}) copy-start(f32[768]{0:T(1024)} %param.37) | copy-start | bytes 9220
  320.1 34.6 %copy-start.67 = (f32[192]{0:T(256)S(1)}, f32[192]{0:T(256)}, u32[]{:S(2)}) copy-start(f32[192]{0:T(256)} %param.35) | copy-start | bytes 2308
  338.8 181.2 %copy-start.34 = (f32[4096]{0:T(1024)}, f32[4096]{0:T(1024)S(1)}, u32[]{:S(2)}) copy-start(f32[4096]{0:T(1024)S(1)} %broadcast_multiply_fusion.1) | copy-start | bytes 49156
  354.7 165.3 %copy-start.37 = (f32[4096]{0:T(1024)}, f32[4096]{0:T(1024)S(1)}, u32[]{:S(2)}) copy-start(f32[4096]{0:T(1024)S(1)} %add_rsqrt_fusion.1) | copy-start | bytes 49156
  354.7 31.3 %copy-start.63 = (bf16[192,768]{1,0:T(8,128)(2,1)S(1)}, bf16[192,768]{1,0:T(8,128)(2,1)}, u32[]{:S(2)}) copy-start(bf16[192,768]{1,0:T(8,128)(2,1)} %param.38) | copy-start | bytes 884740
  354.7 31.3 %copy-start.66 = (f32[192]{0:T(256)S(1)}, f32[192]{0:T(256)}, u32[]{:S(2)}) copy-start(f32[192]{0:T(256)} %param.39) | copy-start | bytes 2308
  390.1 34.5 %copy-start.51 = (f32[192]{0:T(256)S(1)}, f32[192]{0:T(256)}, u32[]{:S(2)}) copy-start(f32[192]{0:T(256)} %param.40) | copy-start | bytes 2308
  424.6 22.0 %copy-start.62 = (f32[192]{0:T(256)S(1)}, f32[192]{0:T(256)}, u32[]{:S(2)}) copy-start(f32[192]{0:T(256)} %param.41) | copy-start | bytes 2308
  446.6 6.1 copy-start.64
  452.7 13.0 %copy-start.16 = (f32[192,4096]{1,0:T(8,128)}, f32[192,4096]{1,0:T(8,128)S(1)}, u32[]{:S(2)}) copy-start(f32[192,4096]{1,0:T(8,128)S(1)} %get-tuple-element.426) | copy-start | bytes 9437188
  511.3 8.7 %copy-start.68 = (f32[192]{0:T(256)S(1)}, f32[192]{0:T(256)}, u32[]{:S(2)}) copy-start(f32[192]{0:T(256)} %param.35) | copy-start | bytes 2308
  516.2 24.9 %collective-permute-start = (bf16[192,4096]{1,0:T(8,128)(2,1)}, bf16[192,4096]{1,0:T(8,128)(2,1)}, u32[]{:S(2)}, u32[]{:S(2)}) collective-permute-start(bf16[192,4096]{1,0:T(8,128)(2,1)} %get-tuple-element.428), channel_id=1, source_target_pairs={{0,1},{1,2},{2,3},{3,0},{4,5},{5,6},{6,7},{7,4},{8,9},{9,10},{10,1... | collective-permute-start | bytes 4718600 | tf_op jit(solution)/shard_map/ppermute | solution.py:232
  516.2 41.6 %collective-permute-start.1 = (bf16[192,4096]{1,0:T(8,128)(2,1)}, bf16[192,4096]{1,0:T(8,128)(2,1)S(1)}, u32[]{:S(2)}, u32[]{:S(2)}) collective-permute-start(bf16[192,4096]{1,0:T(8,128)(2,1)} %get-tuple-element.428), channel_id=1, source_target_pairs={{0,3},{1,0},{2,1},{3,2},{4,7},{5,4},{6,5},{7,6},{8,11},{9,8},{10,9... | collective-permute-start | bytes 4718600 | tf_op jit(solution)/shard_map/ppermute | solution.py:235
  541.1 33.5 %collective-permute-start.2 = (bf16[192,4096]{1,0:T(8,128)(2,1)}, bf16[192,4096]{1,0:T(8,128)(2,1)S(1)}, u32[]{:S(2)}, u32[]{:S(2)}) collective-permute-start(bf16[192,4096]{1,0:T(8,128)(2,1)} %collective-permute-done), channel_id=1, source_target_pairs={{0,1},{1,2},{2,3},{3,0},{4,5},{5,6},{6,7},{7,4},{8,9},{9,10},{10,1... | collective-permute-start | bytes 4718600 | tf_op jit(solution)/shard_map/ppermute | solution.py:232
  551.3 23.5 %copy-start.44 = (bf16[768,192]{0,1:T(8,128)(2,1)S(1)}, bf16[768,192]{0,1:T(8,128)(2,1)}, u32[]{:S(2)}) copy-start(bf16[768,192]{0,1:T(8,128)(2,1)} %param.32) | copy-start | bytes 884740
  613.1 5.7 copy-start.3
  694.4 5.7 copy-start.3
  762.6 25.3 %copy-start.13 = (f32[192,4096]{1,0:T(8,128)S(1)}, f32[192,4096]{1,0:T(8,128)}, u32[]{:S(2)}) copy-start(f32[192,4096]{1,0:T(8,128)} %copy-done.12) | copy-start | bytes 9437188
  762.6 25.3 %copy-start.35 = (f32[4096]{0:T(1024)S(1)}, f32[4096]{0:T(1024)}, u32[]{:S(2)}) copy-start(f32[4096]{0:T(1024)} %copy-done.34) | copy-start | bytes 49156
  762.6 25.3 %copy-start.38 = (f32[4096]{0:T(1024)S(1)}, f32[4096]{0:T(1024)}, u32[]{:S(2)}) copy-start(f32[4096]{0:T(1024)} %copy-done.37) | copy-start | bytes 49156
  762.6 25.3 %copy-start.40 = (bf16[192,192]{1,0:T(8,128)(2,1)S(1)}, bf16[192,192]{1,0:T(8,128)(2,1)}, u32[]{:S(2)}) copy-start(bf16[192,192]{1,0:T(8,128)(2,1)} %param.27) | copy-start | bytes 221188
  762.7 25.3 %copy-start.46 = (f32[4096]{0:T(1024)S(1)}, f32[4096]{0:T(1024)}, u32[]{:S(2)}) copy-start(f32[4096]{0:T(1024)} %copy-done.45) | copy-start | bytes 49156
  762.7 25.3 %copy-start.48 = (f32[4096]{0:T(1024)S(1)}, f32[4096]{0:T(1024)}, u32[]{:S(2)}) copy-start(f32[4096]{0:T(1024)} %copy-done.47) | copy-start | bytes 49156
  762.7 25.3 %copy-start.50 = (f32[192]{0:T(256)S(1)}, f32[192]{0:T(256)}, u32[]{:S(2)}) copy-start(f32[192]{0:T(256)} %param.34) | copy-start | bytes 2308
  793.1 44.4 %copy-start.1 = (bf16[768,192]{0,1:T(8,128)(2,1)S(1)}, bf16[768,192]{0,1:T(8,128)(2,1)}, u32[]{:S(2)}) copy-start(bf16[768,192]{0,1:T(8,128)(2,1)} %param.36) | copy-start | bytes 884740
  827.9 8.7 %copy-start.36 = (f32[192,768]{1,0:T(8,128)S(1)}, f32[192,768]{1,0:T(8,128)}, u32[]{:S(2)}) copy-start(f32[192,768]{1,0:T(8,128)} %get-tuple-element.879) | copy-start | bytes 1769476
  (121 other events, 317.1 us)
Sparse Core Ops, SparseCore 0:
  102.5 214.6 reduce-scatter.3
  765.2 62.6 all-reduce.5
